TPU v7x, 32 devices: a whole 2x2x4 slice. The times are simulated.
32 devices in a mesh: fsdp: 8 (over y, x, core), tp: 4 (over z).
Axes of the slice: x: 2, y: 2, z: 4, core: 2. Of those that a mesh axis runs over, the one named last changes fastest.
Arguments:
- hidden_in: bfloat16 [4096, 2048], P(('fsdp', 'tp')), may hold values from -6 to 6
- cotangent: bfloat16 [4096, 2048], P(('fsdp', 'tp')), may hold values from -6 to 6
- seq_lengths: int32 [8, 4], P('fsdp'), may hold values from 1 to 256, 512 in all within a row
- attn_gain: bfloat16 [2048], P('fsdp'), may hold values from 0.5 to 1.5
- w_query: bfloat16 [2048, 2048], P('fsdp', 'tp'), may hold values from -0.125 to 0.125
- key_weight: bfloat16 [2048, 1024], P('fsdp', 'tp'), may hold values from -0.125 to 0.125
- value_weight: bfloat16 [2048, 1024], P('fsdp', 'tp'), may hold values from -0.125 to 0.125
- q_gain: bfloat16 [128], P('fsdp'), may hold values from 0.5 to 1.5
- k_gain: bfloat16 [128], P('fsdp'), may hold values from 0.5 to 1.5
- w_out: bfloat16 [2048, 2048], P('tp', 'fsdp'), may hold values from -0.5 to 0.5
- mlp_gain: bfloat16 [2048], P('fsdp'), may hold values from 0.5 to 1.5
- w_gate: bfloat16 [2048, 6144], P('fsdp', 'tp'), may hold values from -0.125 to 0.125
- w_up: bfloat16 [2048, 6144], P('fsdp', 'tp'), may hold values from -0.125 to 0.125
- w_down: bfloat16 [6144, 2048], P('tp', 'fsdp'), may hold values from -0.15625 to 0.15625
Outputs:
- block_out: bfloat16 [4096, 2048], P(('fsdp', 'tp'))
- grad_in: bfloat16 [4096, 2048], P(('fsdp', 'tp'))
- grad_attn_gain: float32 [2048], P('fsdp')
- grad_query: float32 [2048, 2048], P('fsdp', 'tp')
- grad_key: float32 [2048, 1024], P('fsdp', 'tp')
- grad_value: float32 [2048, 1024], P('fsdp', 'tp')
- grad_q_gain: float32 [128], P('fsdp')
- grad_k_gain: float32 [128], P('fsdp')
- grad_out_proj: float32 [2048, 2048], P('tp', 'fsdp')
- grad_mlp_gain: float32 [2048], P('fsdp')
- grad_gate: float32 [2048, 6144], P('fsdp', 'tp')
- grad_up: float32 [2048, 6144], P('fsdp', 'tp')
- grad_down: float32 [6144, 2048], P('tp', 'fsdp')
Inputs may be any that keep to these rules, and one draw needn't show every extreme that they name: `seq_lengths`: row s holds the lengths of the sequences packed, in order, in data shard s; each row sums to 512 and its largest entry is exactly 256.
All inputs are finite; a program needn't handle non-finite values.
Results may differ from a plain program's by a relative error of at most 0.025.
Values may be sent and summed in bfloat16 or wider, within the bound.
No kernel may reach another device: no remote copies, remote signals or barrier semaphores. Data moves between devices by JAX's collectives and lax.ppermute only.
A program may use at most 192 MiB of HBM per device.

v0:
```python
import math
import jax
import jax.numpy as jnp
from jax import lax
from jax.sharding import PartitionSpec as P

EPS = 1e-06
THETA = 1000000.0


def positions(lens_row, row_count):
    seq_ends = jnp.cumsum(lens_row)
    token_index = jnp.arange(row_count, dtype=jnp.int32)
    finished = token_index[:, None] >= seq_ends[None, :]
    seq_start = jnp.sum(jnp.where(finished, lens_row[None, :], 0), axis=1)
    return (token_index, seq_start)


def rope_tables(offset, head_width):
    half_width = head_width // 2
    frequency = jnp.exp(
        jnp.arange(half_width, dtype=jnp.float32) * (-2.0 * math.log(THETA) / head_width)
    )
    phase_angle = offset.astype(jnp.float32)[:, None] * frequency[None, :]
    return (jnp.cos(phase_angle)[:, None, :], jnp.sin(phase_angle)[:, None, :])


def rotate(values, cosine, sine):
    half_width = values.shape[-1] // 2
    first_half, second_half = (values[..., :half_width], values[..., half_width:])
    return jnp.concatenate(
        [first_half * cosine - second_half * sine, second_half * cosine + first_half * sine],
        axis=-1,
    )


def unrotate(values, cosine, sine):
    half_width = values.shape[-1] // 2
    first_half, second_half = (values[..., :half_width], values[..., half_width:])
    return jnp.concatenate(
        [first_half * cosine + second_half * sine, second_half * cosine - first_half * sine],
        axis=-1,
    )


def row_norm(values, gain_vec):
    inv_rms = lax.rsqrt(jnp.mean(values * values, axis=-1, keepdims=True) + EPS)
    normed = values * inv_rms
    return (normed * gain_vec.astype(jnp.float32), normed, inv_rms)


def norm_back(incoming, normed, inv_rms, gain_vec):
    scaled = incoming * gain_vec.astype(jnp.float32)
    grad_back = inv_rms * (scaled - normed * jnp.mean(scaled * normed, axis=-1, keepdims=True))
    gain_grad = jnp.sum((incoming * normed).reshape(-1, incoming.shape[-1]), axis=0)
    return (grad_back, gain_grad)


def attend(query_rot, key_rot, value, token_index, seq_start, score_scale):
    row_count, head_count, head_width = query_rot.shape
    kv_heads = key_rot.shape[1]
    groups = head_count // kv_heads
    block_rows = min(512, row_count)
    block_count = row_count // block_rows
    query_block_list = query_rot.reshape(block_count, block_rows, kv_heads, groups, head_width)

    def block_step(block_in):
        query_block, query_pos, query_start = block_in
        scores = (
            jnp.einsum("bkgd,skd->kgbs", query_block, key_rot, preferred_element_type=jnp.float32)
            * score_scale
        )
        allowed = (token_index[None, :] <= query_pos[:, None]) & (
            token_index[None, :] >= query_start[:, None]
        )
        scores = jnp.where(allowed, scores, -1e30)
        row_max = jnp.max(scores, axis=-1, keepdims=True)
        exp_scores = jnp.exp(scores - row_max)
        row_total = jnp.sum(exp_scores, axis=-1, keepdims=True)
        prob_bf = (exp_scores / row_total).astype(jnp.bfloat16)
        block_out = jnp.einsum("kgbs,skd->bkgd", prob_bf, value, preferred_element_type=jnp.float32)
        return (block_out.astype(jnp.bfloat16), (row_max + jnp.log(row_total))[..., 0])

    block_outs, log_sums = lax.map(
        block_step,
        (
            query_block_list,
            token_index.reshape(block_count, block_rows),
            seq_start.reshape(block_count, block_rows),
        ),
    )
    return (block_outs.reshape(row_count, head_count, head_width), log_sums)


def attend_back(
    query_rot, key_rot, value, attended, d_attended, log_sums, token_index, seq_start, score_scale
):
    row_count, head_count, head_width = query_rot.shape
    kv_heads = key_rot.shape[1]
    groups = head_count // kv_heads
    block_rows = min(512, row_count)
    block_count = row_count // block_rows
    shaped = (block_count, block_rows, kv_heads, groups, head_width)

    def block_step(totals, block_in):
        key_grad, value_grad = totals
        query_block, out_block, dout_block, lse_block, query_pos, query_start = block_in
        scores = (
            jnp.einsum("bkgd,skd->kgbs", query_block, key_rot, preferred_element_type=jnp.float32)
            * score_scale
        )
        allowed = (token_index[None, :] <= query_pos[:, None]) & (
            token_index[None, :] >= query_start[:, None]
        )
        probs = jnp.where(allowed, jnp.exp(scores - lse_block[..., None]), 0.0)
        prob_bf = probs.astype(jnp.bfloat16)
        value_grad = value_grad + jnp.einsum(
            "kgbs,bkgd->skd", prob_bf, dout_block, preferred_element_type=jnp.float32
        )
        d_prob = jnp.einsum("bkgd,skd->kgbs", dout_block, value, preferred_element_type=jnp.float32)
        row_delta = jnp.transpose(
            jnp.sum(dout_block.astype(jnp.float32) * out_block.astype(jnp.float32), axis=-1),
            (1, 2, 0),
        )
        d_score = (probs * (d_prob - row_delta[..., None]) * score_scale).astype(jnp.bfloat16)
        query_grad = jnp.einsum(
            "kgbs,skd->bkgd", d_score, key_rot, preferred_element_type=jnp.float32
        )
        key_grad = key_grad + jnp.einsum(
            "kgbs,bkgd->skd", d_score, query_block, preferred_element_type=jnp.float32
        )
        return ((key_grad, value_grad), query_grad)

    empty_kv = jnp.zeros((row_count, kv_heads, head_width), jnp.float32)
    block_in = (
        query_rot.reshape(shaped),
        attended.reshape(shaped),
        d_attended.reshape(shaped),
        log_sums,
        token_index.reshape(block_count, block_rows),
        seq_start.reshape(block_count, block_rows),
    )
    (key_grad, value_grad), query_grads = lax.scan(block_step, (empty_kv, empty_kv), block_in)
    return (query_grads.reshape(row_count, head_count, head_width), key_grad, value_grad)


def local(
    hidden_in,
    cotangent,
    seq_lengths,
    attn_gain,
    w_query,
    key_weight,
    value_weight,
    q_gain,
    k_gain,
    w_out,
    mlp_gain,
    w_gate,
    w_up,
    w_down,
):
    gain_attn, wq_full, wk_full, wv_full, gain_query, gain_key, wo_full = (
        lax.all_gather(attn_gain, "fsdp", axis=0, tiled=True),
        lax.all_gather(w_query, "fsdp", axis=0, tiled=True),
        lax.all_gather(key_weight, "fsdp", axis=0, tiled=True),
        lax.all_gather(value_weight, "fsdp", axis=0, tiled=True),
        lax.all_gather(q_gain, "fsdp", axis=0, tiled=True),
        lax.all_gather(k_gain, "fsdp", axis=0, tiled=True),
        lax.all_gather(w_out, "fsdp", axis=1, tiled=True),
    )
    feedforward_gain, wg_full, wu_full, wd_full = (
        lax.all_gather(mlp_gain, "fsdp", axis=0, tiled=True),
        lax.all_gather(w_gate, "fsdp", axis=0, tiled=True),
        lax.all_gather(w_up, "fsdp", axis=0, tiled=True),
        lax.all_gather(w_down, "fsdp", axis=1, tiled=True),
    )
    head_width = gain_query.shape[0]
    score_scale = 1.0 / math.sqrt(head_width)
    x_float = hidden_in.astype(jnp.float32)
    normed_in, hat_in, inv_in = row_norm(x_float, gain_attn)
    attn_in = lax.all_gather(normed_in.astype(jnp.bfloat16), "tp", axis=0, tiled=True)
    row_count = attn_in.shape[0]
    token_index, seq_start = positions(seq_lengths[0], row_count)
    cosine, sine = rope_tables(token_index - seq_start, head_width)
    query = jnp.dot(attn_in, wq_full, preferred_element_type=jnp.float32).reshape(
        row_count, -1, head_width
    )
    key_proj = jnp.dot(attn_in, wk_full, preferred_element_type=jnp.float32).reshape(
        row_count, -1, head_width
    )
    value = (
        jnp.dot(attn_in, wv_full, preferred_element_type=jnp.float32)
        .astype(jnp.bfloat16)
        .reshape(row_count, -1, head_width)
    )
    q_scaled, q_hat, q_inv = row_norm(query, gain_query)
    k_scaled, k_hat, k_inv = row_norm(key_proj, gain_key)
    query_rot = rotate(q_scaled, cosine, sine).astype(jnp.bfloat16)
    key_rot = rotate(k_scaled, cosine, sine).astype(jnp.bfloat16)
    attended, log_sums = attend(query_rot, key_rot, value, token_index, seq_start, score_scale)
    attended_flat = attended.reshape(row_count, -1)
    residual = x_float + lax.psum_scatter(
        jnp.dot(attended_flat, wo_full, preferred_element_type=jnp.float32),
        "tp",
        scatter_dimension=0,
        tiled=True,
    )
    normed_mid, hat_mid, inv_mid = row_norm(residual, feedforward_gain)
    mlp_in = lax.all_gather(normed_mid.astype(jnp.bfloat16), "tp", axis=0, tiled=True)
    gate_act = jnp.dot(mlp_in, wg_full, preferred_element_type=jnp.float32)
    up_act = jnp.dot(mlp_in, wu_full, preferred_element_type=jnp.float32)
    sigmoid_gate = 1.0 / (1.0 + jnp.exp(-gate_act))
    hidden = (gate_act * sigmoid_gate * up_act).astype(jnp.bfloat16)
    block_out = (
        residual
        + lax.psum_scatter(
            jnp.dot(hidden, wd_full, preferred_element_type=jnp.float32).astype(jnp.bfloat16),
            "tp",
            scatter_dimension=0,
            tiled=True,
        ).astype(jnp.float32)
    ).astype(jnp.bfloat16)
    grad_all = lax.all_gather(cotangent, "tp", axis=0, tiled=True)
    grad_down = jnp.dot(hidden.T, grad_all, preferred_element_type=jnp.float32)
    d_hidden = jnp.dot(grad_all, wd_full.T, preferred_element_type=jnp.float32)
    d_gate = (d_hidden * up_act * sigmoid_gate * (1.0 + gate_act * (1.0 - sigmoid_gate))).astype(
        jnp.bfloat16
    )
    d_up = (d_hidden * gate_act * sigmoid_gate).astype(jnp.bfloat16)
    grad_gate = jnp.dot(mlp_in.T, d_gate, preferred_element_type=jnp.float32)
    grad_up = jnp.dot(mlp_in.T, d_up, preferred_element_type=jnp.float32)
    d_mlp_in = lax.psum_scatter(
        (
            jnp.dot(d_gate, wg_full.T, preferred_element_type=jnp.float32)
            + jnp.dot(d_up, wu_full.T, preferred_element_type=jnp.float32)
        ).astype(jnp.bfloat16),
        "tp",
        scatter_dimension=0,
        tiled=True,
    ).astype(jnp.float32)
    d_mid, grad_gain_mlp = norm_back(d_mlp_in, hat_mid, inv_mid, feedforward_gain)
    d_residual = cotangent.astype(jnp.float32) + d_mid
    d_attn = lax.all_gather(d_residual.astype(jnp.bfloat16), "tp", axis=0, tiled=True)
    grad_out_proj = jnp.dot(attended_flat.T, d_attn, preferred_element_type=jnp.float32)
    d_attended = (
        jnp.dot(d_attn, wo_full.T, preferred_element_type=jnp.float32)
        .astype(jnp.bfloat16)
        .reshape(row_count, -1, head_width)
    )
    dq_rot, dk_rot, d_value = attend_back(
        query_rot,
        key_rot,
        value,
        attended,
        d_attended,
        log_sums,
        token_index,
        seq_start,
        score_scale,
    )
    d_query, grad_gain_query = norm_back(unrotate(dq_rot, cosine, sine), q_hat, q_inv, gain_query)
    d_key, grad_gain_key = norm_back(unrotate(dk_rot, cosine, sine), k_hat, k_inv, gain_key)
    d_query_bf = d_query.reshape(row_count, -1).astype(jnp.bfloat16)
    d_key_bf = d_key.reshape(row_count, -1).astype(jnp.bfloat16)
    d_value_bf = d_value.reshape(row_count, -1).astype(jnp.bfloat16)
    grad_query = jnp.dot(attn_in.T, d_query_bf, preferred_element_type=jnp.float32)
    grad_key = jnp.dot(attn_in.T, d_key_bf, preferred_element_type=jnp.float32)
    grad_value = jnp.dot(attn_in.T, d_value_bf, preferred_element_type=jnp.float32)
    d_attn_in = lax.psum_scatter(
        (
            jnp.dot(d_query_bf, wq_full.T, preferred_element_type=jnp.float32)
            + jnp.dot(d_key_bf, wk_full.T, preferred_element_type=jnp.float32)
            + jnp.dot(d_value_bf, wv_full.T, preferred_element_type=jnp.float32)
        ).astype(jnp.bfloat16),
        "tp",
        scatter_dimension=0,
        tiled=True,
    ).astype(jnp.float32)
    d_in_norm, grad_gain_attn = norm_back(d_attn_in, hat_in, inv_in, gain_attn)
    grad_in = (d_residual + d_in_norm).astype(jnp.bfloat16)
    every_sum = (
        lax.psum_scatter(
            grad_gain_attn.astype(jnp.bfloat16), "fsdp", scatter_dimension=0, tiled=True
        ).astype(jnp.float32),
        lax.psum_scatter(
            grad_query.astype(jnp.bfloat16), "fsdp", scatter_dimension=0, tiled=True
        ).astype(jnp.float32),
        lax.psum_scatter(
            grad_key.astype(jnp.bfloat16), "fsdp", scatter_dimension=0, tiled=True
        ).astype(jnp.float32),
        lax.psum_scatter(
            grad_value.astype(jnp.bfloat16), "fsdp", scatter_dimension=0, tiled=True
        ).astype(jnp.float32),
        lax.psum_scatter(
            grad_gain_query.astype(jnp.bfloat16), "fsdp", scatter_dimension=0, tiled=True
        ).astype(jnp.float32),
        lax.psum_scatter(
            grad_gain_key.astype(jnp.bfloat16), "fsdp", scatter_dimension=0, tiled=True
        ).astype(jnp.float32),
        lax.psum_scatter(
            grad_out_proj.astype(jnp.bfloat16), "fsdp", scatter_dimension=1, tiled=True
        ).astype(jnp.float32),
        lax.psum_scatter(
            grad_gain_mlp.astype(jnp.bfloat16), "fsdp", scatter_dimension=0, tiled=True
        ).astype(jnp.float32),
        lax.psum_scatter(
            grad_gate.astype(jnp.bfloat16), "fsdp", scatter_dimension=0, tiled=True
        ).astype(jnp.float32),
        lax.psum_scatter(
            grad_up.astype(jnp.bfloat16), "fsdp", scatter_dimension=0, tiled=True
        ).astype(jnp.float32),
        lax.psum_scatter(
            grad_down.astype(jnp.bfloat16), "fsdp", scatter_dimension=1, tiled=True
        ).astype(jnp.float32),
    )
    attn_sums = every_sum[:7]
    mlp_sums = every_sum[7:]
    gain_totals = lax.psum((attn_sums[0], attn_sums[4], attn_sums[5], mlp_sums[0]), "tp")
    return (
        block_out,
        grad_in,
        gain_totals[0],
        attn_sums[1],
        attn_sums[2],
        attn_sums[3],
        gain_totals[1],
        gain_totals[2],
        attn_sums[6],
        gain_totals[3],
        mlp_sums[1],
        mlp_sums[2],
        mlp_sums[3],
    )


def solution(mesh):
    return jax.shard_map(
        local,
        mesh=mesh,
        in_specs=(
            P(("fsdp", "tp"), None),
            P(("fsdp", "tp"), None),
            P("fsdp", None),
            P("fsdp"),
            P("fsdp", "tp"),
            P("fsdp", "tp"),
            P("fsdp", "tp"),
            P("fsdp"),
            P("fsdp"),
            P("tp", "fsdp"),
            P("fsdp"),
            P("fsdp", "tp"),
            P("fsdp", "tp"),
            P("tp", "fsdp"),
        ),
        out_specs=(
            P(("fsdp", "tp"), None),
            P(("fsdp", "tp"), None),
            P("fsdp"),
            P("fsdp", "tp"),
            P("fsdp", "tp"),
            P("fsdp", "tp"),
            P("fsdp"),
            P("fsdp"),
            P("tp", "fsdp"),
            P("fsdp"),
            P("fsdp", "tp"),
            P("fsdp", "tp"),
            P("tp", "fsdp"),
        ),
        check_vma=False,
    )
```

profile of v0, /device:TPU:0, one launch (start us, length us, event | category | flops | bytes accessed | tf_op | source)
XLA Modules:
  0.0 1075.7 jit_solution(12785175896997641999)
XLA Ops:
  8.7 10.4 all-gather
  27.8 13.5 %all-reduce.8 = (bf16[128]{0:T(256)(128)(2,1)S(1)}, bf16[128]{0:T(256)(128)(2,1)S(1)}) all-reduce(bf16[128]{0:T(256)(128)(2,1)S(1)} %dynamic-update-slice.1, bf16[128]{0:T(256)(128)(2,1)S(1)} %dynamic-update-slice), channel_id=1, replica_groups=mesh['fsdp'=8,'tp'=4] {'fsdp'}, use_global_device_ids=true, to_apply=%add.1 | all-reduce | flops 256 | bytes 1024
  42.3 41.6 %all-gather.14.cloned.1.call-done = bf16[512,2048]{1,0:T(8,128)(2,1)} async-done(((bf16[128,2048]{1,0:T(8,128)(2,1)}), bf16[512,2048]{1,0:T(8,128)(2,1)}) %all-gather.14.cloned.1.call-update) | async-done | bytes 2097168 | tf_op jit(solution)/shard_map/all_gather | solution.py:182
  88.1 20.0 %all-gather.16.cloned.1.call-done = bf16[2048,256]{1,0:T(8,128)(2,1)} async-done(((bf16[256,256]{1,0:T(8,128)(2,1)}), bf16[2048,256]{1,0:T(8,128)(2,1)}) %all-gather.16.cloned.1.call-update) | async-done | bytes 1048592 | tf_op jit(solution)/shard_map/all_gather | solution.py:167
  111.4 26.2 %all-gather.20.cloned.1.call-done = bf16[2048,512]{1,0:T(8,128)(2,1)} async-done(((bf16[256,512]{1,0:T(8,128)(2,1)}), bf16[2048,512]{1,0:T(8,128)(2,1)}) %all-gather.20.cloned.1.call-update) | async-done | bytes 2097168 | tf_op jit(solution)/shard_map/all_gather | solution.py:165
  148.4 19.1 %all-gather.22.cloned.1.call-done = bf16[512,2048]{1,0:T(8,128)(2,1)} async-done(((bf16[512,256]{1,0:T(8,128)(2,1)}), bf16[512,2048]{1,0:T(8,128)(2,1)}) %all-gather.22.cloned.1.call-update) | async-done | bytes 2097168 | tf_op jit(solution)/shard_map/all_gather | solution.py:170
  182.1 67.2 %reduce-scatter.12.cloned.1.call-done = f32[128,2048]{1,0:T(8,128)} async-done(((f32[512,2048]{1,0:T(8,128)}), f32[128,2048]{1,0:T(8,128)}) %reduce-scatter.12.cloned.1.call-update) | async-done | bytes 1048592 | tf_op jit(solution)/shard_map/reduce_scatter | solution.py:203
  254.0 43.1 %all-gather.26.cloned.1.call-done = bf16[2048,1536]{1,0:T(8,128)(2,1)} async-done(((bf16[256,1536]{1,0:T(8,128)(2,1)}), bf16[2048,1536]{1,0:T(8,128)(2,1)}) %all-gather.26.cloned.1.call-update) | async-done | bytes 6291472 | tf_op jit(solution)/shard_map/all_gather | solution.py:174
  297.1 47.8 %all-gather.24.cloned.1.call-done = bf16[512,2048]{1,0:T(8,128)(2,1)} async-done(((bf16[128,2048]{1,0:T(8,128)(2,1)}), bf16[512,2048]{1,0:T(8,128)(2,1)}) %all-gather.24.cloned.1.call-update) | async-done | bytes 2097168 | tf_op jit(solution)/shard_map/all_gather | solution.py:210
  353.5 37.6 %all-gather.28.cloned.1.call-done = bf16[2048,1536]{1,0:T(8,128)(2,1)} async-done(((bf16[256,1536]{1,0:T(8,128)(2,1)}), bf16[2048,1536]{1,0:T(8,128)(2,1)}) %all-gather.28.cloned.1.call-update) | async-done | bytes 6291472 | tf_op jit(solution)/shard_map/all_gather | solution.py:175
  399.6 38.5 %all-gather.32.cloned.1.call-done = bf16[512,2048]{1,0:T(8,128)(2,1)} async-done(((bf16[128,2048]{1,0:T(8,128)(2,1)}), bf16[512,2048]{1,0:T(8,128)(2,1)}) %all-gather.32.cloned.1.call-update) | async-done | bytes 2097168 | tf_op jit(solution)/shard_map/all_gather | solution.py:224
  438.2 47.3 %all-gather.30.cloned.1.call-done = bf16[1536,2048]{1,0:T(8,128)(2,1)} async-done(((bf16[1536,256]{1,0:T(8,128)(2,1)}), bf16[1536,2048]{1,0:T(8,128)(2,1)}) %all-gather.30.cloned.1.call-update) | async-done | bytes 6291472 | tf_op jit(solution)/shard_map/all_gather | solution.py:176
  485.5 11.0 %multiply_convert_fusion = (bf16[512,1536]{1,0:T(8,128)(2,1)S(1)}, bf16[512,1536]{1,0:T(8,128)(2,1)S(1)}, bf16[512,1536]{1,0:T(8,128)(2,1)}) fusion(f32[512,1536]{1,0:T(8,128)} %fusion.59, f32[512,1536]{1,0:T(8,128)} %fusion.60, bf16[512,2048]{1,0:T(8,128)(2,1)} %all-gather.32.cloned.1.call-done, bf16[1536,2048]{1,0:T(8,128)(2,1)} %all-gather.30.cloned.1.call-done), kind=kOutput, calls=%fused_computation.18 | convolution fusion | flops 3233808384 | bytes 19398656 | tf_op jit(solution)/shard_map/dot_general | solution.py:226
  508.1 43.7 %reduce-scatter.16.cloned.1.call-done = bf16[128,2048]{1,0:T(8,128)(2,1)} async-done(((bf16[512,2048]{1,0:T(8,128)(2,1)}), bf16[128,2048]{1,0:T(8,128)(2,1)}) %reduce-scatter.16.cloned.1.call-update) | async-done | bytes 524304 | tf_op jit(solution)/shard_map/reduce_scatter | solution.py:233
  555.9 44.7 %all-gather.34.cloned.1.call-done = bf16[512,2048]{1,0:T(8,128)(2,1)} async-done(((bf16[128,2048]{1,0:T(8,128)(2,1)}), bf16[512,2048]{1,0:T(8,128)(2,1)}) %all-gather.34.cloned.1.call-update) | async-done | bytes 2097168 | tf_op jit(solution)/shard_map/all_gather | solution.py:244
  708.7 47.3 %reduce-scatter.28.cloned.1.call-done = bf16[256,1536]{1,0:T(8,128)(2,1)} async-done(((bf16[2048,1536]{1,0:T(8,128)(2,1)}), bf16[256,1536]{1,0:T(8,128)(2,1)}) %reduce-scatter.28.cloned.1.call-update) | async-done | bytes 786448 | tf_op jit(solution)/shard_map/reduce_scatter | solution.py:307
  758.4 62.6 %reduce-scatter.30.cloned.1.call-done = bf16[256,1536]{1,0:T(8,128)(2,1)} async-done(((bf16[2048,1536]{1,0:T(8,128)(2,1)}), bf16[256,1536]{1,0:T(8,128)(2,1)}) %reduce-scatter.30.cloned.1.call-update) | async-done | bytes 786448 | tf_op jit(solution)/shard_map/reduce_scatter | solution.py:310
  823.5 62.4 %reduce-scatter.32.cloned.1.call-done = bf16[1536,256]{1,0:T(8,128)(2,1)} async-done(((bf16[1536,2048]{1,0:T(8,128)(2,1)}), bf16[1536,256]{1,0:T(8,128)(2,1)}) %reduce-scatter.32.cloned.1.call-update) | async-done | bytes 786448 | tf_op jit(solution)/shard_map/reduce_scatter | solution.py:313
  888.2 42.0 %reduce-scatter.20.cloned.1.call-done = bf16[256,512]{1,0:T(8,128)(2,1)} async-done(((bf16[2048,512]{1,0:T(8,128)(2,1)}), bf16[256,512]{1,0:T(8,128)(2,1)}) %reduce-scatter.20.cloned.1.call-update) | async-done | bytes 262160 | tf_op jit(solution)/shard_map/reduce_scatter | solution.py:286
  932.1 42.5 %reduce-scatter.26.cloned.1.call-done = bf16[512,256]{1,0:T(8,128)(2,1)} async-done(((bf16[512,2048]{1,0:T(8,128)(2,1)}), bf16[512,256]{1,0:T(8,128)(2,1)}) %reduce-scatter.26.cloned.1.call-update) | async-done | bytes 262160 | tf_op jit(solution)/shard_map/reduce_scatter | solution.py:301
  976.3 44.2 %reduce-scatter.18.cloned.1.call-done = bf16[128,2048]{1,0:T(8,128)(2,1)} async-done(((bf16[512,2048]{1,0:T(8,128)(2,1)}), bf16[128,2048]{1,0:T(8,128)(2,1)}) %reduce-scatter.18.cloned.1.call-update) | async-done | bytes 524304 | tf_op jit(solution)/shard_map/reduce_scatter | solution.py:270
  1022.0 13.8 %all-reduce.7 = (bf16[2048]{0:T(1024)(128)(2,1)S(1)}, bf16[128]{0:T(256)(128)(2,1)S(1)}, bf16[128]{0:T(256)(128)(2,1)S(1)}, bf16[2048]{0:T(1024)(128)(2,1)S(1)}) all-reduce(bf16[2048]{0:T(1024)(128)(2,1)S(1)} %get-tuple-element.68, bf16[128]{0:T(256)(128)(2,1)S(1)} %fusion.40, ...), channel_id=6, replica_groups=mesh['fsdp'=8,'tp'=4] {'fsdp'}, use_global_device_ids=true, to_apply=%region_18.19.clone | all-reduce | flops 4352 | bytes 17408
  1035.9 11.8 %all-reduce.6 = (f32[256]{0:T(256)}, f32[16]{0:T(128)}, f32[16]{0:T(128)}, f32[256]{0:T(256)}) all-reduce(f32[256]{0:T(256)S(1)} %get-tuple-element.127, f32[16]{0:T(128)S(1)} %get-tuple-element.129, f32[16]{0:T(128)S(1)} %get-tuple-element.128, f32[256]{0:T(256)S(1)} %get-tuple-element.126), channel_id=1, replica_groups=mesh['fsdp'=8,'tp'=4] {'tp'}, use_global_device_ids=true, to_apply=%region_19.20 | all-reduce | flops 544 | bytes 4352 | tf_op jit(solution)/shard_map/psum | solution.py:319
  1047.8 18.1 %reduce-scatter.14.cloned.1.call-done = bf16[128,2048]{1,0:T(8,128)(2,1)} async-done(((bf16[512,2048]{1,0:T(8,128)(2,1)}), bf16[128,2048]{1,0:T(8,128)(2,1)}) %reduce-scatter.14.cloned.1.call-update) | async-done | bytes 524304 | tf_op jit(solution)/shard_map/reduce_scatter | solution.py:217
  (251 shorter events, 201.8 us)
Async XLA Ops:
  7.2 35.1 %all-gather.18.cloned.1.call-start = ((), (), s32[]{:S(2)}) async-start(), calls=%async_computation.13 | async-start | bytes 1179648 | tf_op jit(solution)/shard_map/all_gather | solution.py:166
  7.9 76.0 %all-gather.14.cloned.1.call-start = ((), (), s32[]{:S(2)}) async-start(), calls=%async_computation.11 | async-start | bytes 2621440 | tf_op jit(solution)/shard_map/all_gather | solution.py:182
  22.4 85.7 %all-gather.16.cloned.1.call-start = ((), (), s32[]{:S(2)}) async-start(), calls=%async_computation.12 | async-start | bytes 1179648 | tf_op jit(solution)/shard_map/all_gather | solution.py:167
  23.1 114.5 %all-gather.20.cloned.1.call-start = ((), (), s32[]{:S(2)}) async-start(), calls=%async_computation.14 | async-start | bytes 2359296 | tf_op jit(solution)/shard_map/all_gather | solution.py:165
  23.7 143.8 %all-gather.22.cloned.1.call-start = ((), (), s32[]{:S(2)}) async-start(), calls=%async_computation.15 | async-start | bytes 2359296 | tf_op jit(solution)/shard_map/all_gather | solution.py:170
  24.3 225.0 %reduce-scatter.12.cloned.1.call-start = ((), (), s32[]{:S(2)}) async-start(), calls=%async_computation.16 | async-start | bytes 5242880 | tf_op jit(solution)/shard_map/reduce_scatter | solution.py:203
  172.4 124.8 %all-gather.26.cloned.1.call-start = ((), (), s32[]{:S(2)}) async-start(), calls=%async_computation.18 | async-start | bytes 7077888 | tf_op jit(solution)/shard_map/all_gather | solution.py:174
  173.1 171.8 %all-gather.24.cloned.1.call-start = ((), (), s32[]{:S(2)}) async-start(), calls=%async_computation.17 | async-start | bytes 2621440 | tf_op jit(solution)/shard_map/all_gather | solution.py:210
  251.7 139.3 %all-gather.28.cloned.1.call-start = ((), (), s32[]{:S(2)}) async-start(), calls=%async_computation.19 | async-start | bytes 7077888 | tf_op jit(solution)/shard_map/all_gather | solution.py:175
  252.5 185.7 %all-gather.32.cloned.1.call-start = ((), (), s32[]{:S(2)}) async-start(), calls=%async_computation.22 | async-start | bytes 2621440 | tf_op jit(solution)/shard_map/all_gather | solution.py:224
  253.1 232.4 %all-gather.30.cloned.1.call-start = ((), (), s32[]{:S(2)}) async-start(), calls=%async_computation.20 | async-start | bytes 7077888 | tf_op jit(solution)/shard_map/all_gather | solution.py:176
  253.8 298.0 %reduce-scatter.16.cloned.1.call-start = ((), (), s32[]{:S(2)}) async-start(), calls=%async_computation.23 | async-start | bytes 2621440 | tf_op jit(solution)/shard_map/reduce_scatter | solution.py:233
  508.0 92.6 %all-gather.34.cloned.1.call-start = ((), (), s32[]{:S(2)}) async-start(), calls=%async_computation.24 | async-start | bytes 2621440 | tf_op jit(solution)/shard_map/all_gather | solution.py:244
  555.6 149.8 %reduce-scatter.22.cloned.1.call-start = ((), (), s32[]{:S(2)}) async-start(), calls=%async_computation.27 | async-start | bytes 1179648 | tf_op jit(solution)/shard_map/reduce_scatter | solution.py:289
  617.0 90.0 %reduce-scatter.24.cloned.1.call-start = ((), (), s32[]{:S(2)}) async-start(), calls=%async_computation.28 | async-start | bytes 1179648 | tf_op jit(solution)/shard_map/reduce_scatter | solution.py:292
  623.1 132.9 %reduce-scatter.28.cloned.1.call-start = ((), (), s32[]{:S(2)}) async-start(), calls=%async_computation.30 | async-start | bytes 7077888 | tf_op jit(solution)/shard_map/reduce_scatter | solution.py:307
  631.5 189.5 %reduce-scatter.30.cloned.1.call-start = ((), (), s32[]{:S(2)}) async-start(), calls=%async_computation.31 | async-start | bytes 7077888 | tf_op jit(solution)/shard_map/reduce_scatter | solution.py:310
  640.1 245.8 %reduce-scatter.32.cloned.1.call-start = ((), (), s32[]{:S(2)}) async-start(), calls=%async_computation.32 | async-start | bytes 7077888 | tf_op jit(solution)/shard_map/reduce_scatter | solution.py:313
  648.4 281.9 %reduce-scatter.20.cloned.1.call-start = ((), (), s32[]{:S(2)}) async-start(), calls=%async_computation.26 | async-start | bytes 2359296 | tf_op jit(solution)/shard_map/reduce_scatter | solution.py:286
  671.7 302.8 %reduce-scatter.26.cloned.1.call-start = ((), (), s32[]{:S(2)}) async-start(), calls=%async_computation.29 | async-start | bytes 2359296 | tf_op jit(solution)/shard_map/reduce_scatter | solution.py:301
  676.2 344.3 %reduce-scatter.18.cloned.1.call-start = ((), (), s32[]{:S(2)}) async-start(), calls=%async_computation.25 | async-start | bytes 2621440 | tf_op jit(solution)/shard_map/reduce_scatter | solution.py:270
  682.7 383.2 %reduce-scatter.14.cloned.1.call-start = ((), (), s32[]{:S(2)}) async-start(), calls=%async_computation.21 | async-start | bytes 2621440 | tf_op jit(solution)/shard_map/reduce_scatter | solution.py:217
  758.4 307.5 %copy-start.10 = (bf16[128,2048]{1,0:T(8,128)(2,1)S(1)}, bf16[128,2048]{1,0:T(8,128)(2,1)}, u32[]{:S(2)}) copy-start(bf16[128,2048]{1,0:T(8,128)(2,1)} %param.15) | copy-start | bytes 1572868
  758.4 307.5 %copy-start.18 = (bf16[128,2048]{1,0:T(8,128)(2,1)S(1)}, bf16[128,2048]{1,0:T(8,128)(2,1)}, u32[]{:S(2)}) copy-start(bf16[128,2048]{1,0:T(8,128)(2,1)} %reduce-scatter.16.cloned.1.call-done) | copy-start | bytes 1572868
  (47 other events, 347.1 us)
Sparse Core Ops, SparseCore 0:
  9.9 26.1 all-gather.17
  38.2 45.6 all-gather.13
  85.9 22.1 all-gather.15
  109.8 27.7 all-gather.19
  139.3 28.0 all-gather.21
  172.5 76.7 reduce-scatter.11
  251.2 45.8 all-gather.25
  299.2 45.6 all-gather.23
  346.8 44.1 all-gather.27
  392.5 45.6 all-gather.31
  440.0 45.3 all-gather.29
  508.1 43.5 reduce-scatter.15
  555.7 44.8 all-gather.33
  617.1 34.7 reduce-scatter.21
  654.9 35.9 reduce-scatter.23
  694.2 61.7 reduce-scatter.27
  759.2 61.7 reduce-scatter.29
  824.2 61.5 reduce-scatter.31
  889.1 41.0 reduce-scatter.19
  933.4 41.0 reduce-scatter.25
  976.8 43.6 reduce-scatter.17
  1022.8 43.0 reduce-scatter.13
where the time goes:
time: 1090 us; the launch traced here: 1080 us
  waiting for transfers between devices  801 us (73%)
  matrix products  121 us (11%)
  blocking collectives  58.4 us (5%)
  other arithmetic  46.5 us (4%)
  local copies, waits for them, and re-layouts  29.7 us (3%)
  between operations  17.4 us (2%)
    reduce_scatter x1, waiting for transfers between devices, local(): lax.psum_scatter(jnp.dot(attended_flat, wo_full, preferred_element_type=j...  67.2 us
    reduce_scatter x1, waiting for transfers between devices, local(): lax.psum_scatter(grad_up.astype(jnp.bfloat16), 'fsdp', scatter_dimension=...  62.6 us
    reduce_scatter x1, waiting for transfers between devices, local(): lax.psum_scatter(grad_down.astype(jnp.bfloat16), 'fsdp', scatter_dimensio...  62.4 us
    all_gather x1, waiting for transfers between devices, local(): lax.all_gather(normed_mid.astype(jnp.bfloat16), 'tp', axis=0, tiled=True)  47.8 us
    all_gather x1, waiting for transfers between devices, local(): lax.all_gather(w_down, 'fsdp', axis=1, tiled=True)  47.3 us
    reduce_scatter x1, waiting for transfers between devices, local(): lax.psum_scatter(grad_gate.astype(jnp.bfloat16), 'fsdp', scatter_dimensio...  47.3 us
    all_gather x1, waiting for transfers between devices, local(): lax.all_gather(d_residual.astype(jnp.bfloat16), 'tp', axis=0, tiled=True)  44.7 us
    reduce_scatter x1, waiting for transfers between devices, local(): lax.psum_scatter((jnp.dot(d_query_bf, wq_full.T, preferred_element_type=j...  44.2 us
  transfers between devices with their start and end apart: 22, of which 19 were waited for; matrix products, arithmetic and copies ran while one was open for 13% of the time, Pallas kernels for 0%

commit v1 on v0

--- a/solution.py
+++ b/solution.py
@@ -3,6 +3,7 @@
 import jax.numpy as jnp
 from jax import lax
 from jax.sharding import PartitionSpec as P
+from jax.lax import all_to_all, psum
 
 EPS = 1e-06
 THETA = 1000000.0
@@ -207,7 +208,11 @@
         tiled=True,
     )
     normed_mid, hat_mid, inv_mid = row_norm(residual, feedforward_gain)
-    mlp_in = lax.all_gather(normed_mid.astype(jnp.bfloat16), "tp", axis=0, tiled=True)
+    m = normed_mid.astype(jnp.bfloat16)
+    by_place = []
+    for _ in range(psum(1, axis_name="tp")):
+        by_place.append(m)
+    mlp_in = jnp.concatenate(all_to_all(jnp.stack(by_place, 0), "tp", 0, 0), 0)
     gate_act = jnp.dot(mlp_in, wg_full, preferred_element_type=jnp.float32)
     up_act = jnp.dot(mlp_in, wu_full, preferred_element_type=jnp.float32)
     sigmoid_gate = 1.0 / (1.0 + jnp.exp(-gate_act))

time: 1090 us -> 1040 us (0.954)
  waiting for transfers between devices: 801 us -> 751 us
    all_gather x1 -> x0, waiting for transfers between devices: 47.8 us -> none  [local(): lax.all_gather(normed_mid.astype(jnp.bfloat16), 'tp', axis=0, tiled=True)]
  transfers between devices with their start and end apart: 22 -> 22, of which waited for: 19 -> 19; matrix products, arithmetic and copies ran while one was open for 13% -> 14% of each run, Pallas kernels for 0% -> 0%
where the time goes in v1:
time: 1040 us; the launch traced here: 1030 us
  waiting for transfers between devices  751 us (72%)
  matrix products  121 us (12%)
  blocking collectives  58.3 us (6%)
  other arithmetic  45.1 us (4%)
  local copies, waits for them, and re-layouts  30.1 us (3%)
  between operations  17.4 us (2%)
    reduce_scatter x1, waiting for transfers between devices, local(): lax.psum_scatter(jnp.dot(attended_flat, wo_full, preferred_element_type=j...  65.2 us
    reduce_scatter x1, waiting for transfers between devices, local(): lax.psum_scatter(grad_up.astype(jnp.bfloat16), 'fsdp', scatter_dimension=...  62.6 us
    reduce_scatter x1, waiting for transfers between devices, local(): lax.psum_scatter(grad_down.astype(jnp.bfloat16), 'fsdp', scatter_dimensio...  62.4 us
    reduce_scatter x1, waiting for transfers between devices, local(): lax.psum_scatter(grad_gate.astype(jnp.bfloat16), 'fsdp', scatter_dimensio...  49.2 us
    all_gather x1, waiting for transfers between devices, local(): lax.all_gather(w_down, 'fsdp', axis=1, tiled=True)  47.1 us
    all_gather x1, waiting for transfers between devices, local(): lax.all_gather(d_residual.astype(jnp.bfloat16), 'tp', axis=0, tiled=True)  44.7 us
    reduce_scatter x1, waiting for transfers between devices, local(): lax.psum_scatter((jnp.dot(d_query_bf, wq_full.T, preferred_element_type=j...  44 us
    reduce_scatter x1, waiting for transfers between devices, local(): lax.psum_scatter((jnp.dot(d_gate, wg_full.T, preferred_element_type=jnp.f...  43.7 us
  transfers between devices with their start and end apart: 22, of which 19 were waited for; matrix products, arithmetic and copies ran while one was open for 14% of the time, Pallas kernels for 0%

profile of v1, /device:TPU:0, one launch (start us, length us, event | category | flops | bytes accessed | tf_op | source)
XLA Modules:
  0.0 1029.1 jit_solution(8437211736208437760)
XLA Ops:
  8.7 10.4 %all-gather = bf16[8,1,256]{2,1,0:T(2,128)(2,1)S(1)} all-gather(bf16[1,1,256]{2,1,0:T(2,128)(2,1)S(1)} %reshape.271), channel_id=1, replica_groups=mesh['fsdp'=8,'tp'=4] {'fsdp'}, dimensions={0}, use_global_device_ids=true | all-gather | bytes 4608 | tf_op jit(solution)/shard_map/all_gather | solution.py:165
  27.8 13.5 %all-reduce.8 = (bf16[128]{0:T(256)(128)(2,1)S(1)}, bf16[128]{0:T(256)(128)(2,1)S(1)}) all-reduce(bf16[128]{0:T(256)(128)(2,1)S(1)} %dynamic-update-slice.1, bf16[128]{0:T(256)(128)(2,1)S(1)} %dynamic-update-slice), channel_id=1, replica_groups=mesh['fsdp'=8,'tp'=4] {'fsdp'}, use_global_device_ids=true, to_apply=%add.1 | all-reduce | flops 256 | bytes 1024
  42.3 41.6 %all-gather.13.cloned.1.call-done = bf16[512,2048]{1,0:T(8,128)(2,1)} async-done(((bf16[128,2048]{1,0:T(8,128)(2,1)}), bf16[512,2048]{1,0:T(8,128)(2,1)}) %all-gather.13.cloned.1.call-update) | async-done | bytes 2097168 | tf_op jit(solution)/shard_map/all_gather | solution.py:183
  88.1 20.0 %all-gather.15.cloned.1.call-done = bf16[2048,256]{1,0:T(8,128)(2,1)} async-done(((bf16[256,256]{1,0:T(8,128)(2,1)}), bf16[2048,256]{1,0:T(8,128)(2,1)}) %all-gather.15.cloned.1.call-update) | async-done | bytes 1048592 | tf_op jit(solution)/shard_map/all_gather | solution.py:168
  111.4 26.2 %all-gather.19.cloned.1.call-done = bf16[2048,512]{1,0:T(8,128)(2,1)} async-done(((bf16[256,512]{1,0:T(8,128)(2,1)}), bf16[2048,512]{1,0:T(8,128)(2,1)}) %all-gather.19.cloned.1.call-update) | async-done | bytes 2097168 | tf_op jit(solution)/shard_map/all_gather | solution.py:166
  148.4 19.1 %all-gather.21.cloned.1.call-done = bf16[512,2048]{1,0:T(8,128)(2,1)} async-done(((bf16[512,256]{1,0:T(8,128)(2,1)}), bf16[512,2048]{1,0:T(8,128)(2,1)}) %all-gather.21.cloned.1.call-update) | async-done | bytes 2097168 | tf_op jit(solution)/shard_map/all_gather | solution.py:171
  184.2 65.2 %reduce-scatter.12.cloned.1.call-done = f32[128,2048]{1,0:T(8,128)} async-done(((f32[512,2048]{1,0:T(8,128)}), f32[128,2048]{1,0:T(8,128)}) %reduce-scatter.12.cloned.1.call-update) | async-done | bytes 1048592 | tf_op jit(solution)/shard_map/reduce_scatter | solution.py:204
  257.4 39.8 %all-gather.23.cloned.1.call-done = bf16[2048,1536]{1,0:T(8,128)(2,1)} async-done(((bf16[256,1536]{1,0:T(8,128)(2,1)}), bf16[2048,1536]{1,0:T(8,128)(2,1)}) %all-gather.23.cloned.1.call-update) | async-done | bytes 6291472 | tf_op jit(solution)/shard_map/all_gather | solution.py:175
  305.9 9.0 fusion.59
  314.9 29.6 %all-gather.25.cloned.1.call-done = bf16[2048,1536]{1,0:T(8,128)(2,1)} async-done(((bf16[256,1536]{1,0:T(8,128)(2,1)}), bf16[2048,1536]{1,0:T(8,128)(2,1)}) %all-gather.25.cloned.1.call-update) | async-done | bytes 6291472 | tf_op jit(solution)/shard_map/all_gather | solution.py:176
  353.1 38.7 %all-gather.29.cloned.1.call-done = bf16[512,2048]{1,0:T(8,128)(2,1)} async-done(((bf16[128,2048]{1,0:T(8,128)(2,1)}), bf16[512,2048]{1,0:T(8,128)(2,1)}) %all-gather.29.cloned.1.call-update) | async-done | bytes 2097168 | tf_op jit(solution)/shard_map/all_gather | solution.py:229
  391.8 47.1 %all-gather.27.cloned.1.call-done = bf16[1536,2048]{1,0:T(8,128)(2,1)} async-done(((bf16[1536,256]{1,0:T(8,128)(2,1)}), bf16[1536,2048]{1,0:T(8,128)(2,1)}) %all-gather.27.cloned.1.call-update) | async-done | bytes 6291472 | tf_op jit(solution)/shard_map/all_gather | solution.py:177
  438.9 11.0 %multiply_convert_fusion = (bf16[512,1536]{1,0:T(8,128)(2,1)S(1)}, bf16[512,1536]{1,0:T(8,128)(2,1)S(1)}, bf16[512,1536]{1,0:T(8,128)(2,1)}) fusion(f32[512,1536]{1,0:T(8,128)} %fusion.59, f32[512,1536]{1,0:T(8,128)} %fusion.60, bf16[512,2048]{1,0:T(8,128)(2,1)} %all-gather.29.cloned.1.call-done, bf16[1536,2048]{1,0:T(8,128)(2,1)} %all-gather.27.cloned.1.call-done), kind=kOutput, calls=%fused_computation.18 | convolution fusion | flops 3233808384 | bytes 19398656 | tf_op jit(solution)/shard_map/dot_general | solution.py:231
  461.5 43.7 %reduce-scatter.16.cloned.1.call-done = bf16[128,2048]{1,0:T(8,128)(2,1)} async-done(((bf16[512,2048]{1,0:T(8,128)(2,1)}), bf16[128,2048]{1,0:T(8,128)(2,1)}) %reduce-scatter.16.cloned.1.call-update) | async-done | bytes 524304 | tf_op jit(solution)/shard_map/reduce_scatter | solution.py:238
  509.4 44.7 %all-gather.31.cloned.1.call-done = bf16[512,2048]{1,0:T(8,128)(2,1)} async-done(((bf16[128,2048]{1,0:T(8,128)(2,1)}), bf16[512,2048]{1,0:T(8,128)(2,1)}) %all-gather.31.cloned.1.call-update) | async-done | bytes 2097168 | tf_op jit(solution)/shard_map/all_gather | solution.py:249
  660.4 49.2 %reduce-scatter.28.cloned.1.call-done = bf16[256,1536]{1,0:T(8,128)(2,1)} async-done(((bf16[2048,1536]{1,0:T(8,128)(2,1)}), bf16[256,1536]{1,0:T(8,128)(2,1)}) %reduce-scatter.28.cloned.1.call-update) | async-done | bytes 786448 | tf_op jit(solution)/shard_map/reduce_scatter | solution.py:312
  712.0 62.6 %reduce-scatter.30.cloned.1.call-done = bf16[256,1536]{1,0:T(8,128)(2,1)} async-done(((bf16[2048,1536]{1,0:T(8,128)(2,1)}), bf16[256,1536]{1,0:T(8,128)(2,1)}) %reduce-scatter.30.cloned.1.call-update) | async-done | bytes 786448 | tf_op jit(solution)/shard_map/reduce_scatter | solution.py:315
  777.0 62.4 %reduce-scatter.32.cloned.1.call-done = bf16[1536,256]{1,0:T(8,128)(2,1)} async-done(((bf16[1536,2048]{1,0:T(8,128)(2,1)}), bf16[1536,256]{1,0:T(8,128)(2,1)}) %reduce-scatter.32.cloned.1.call-update) | async-done | bytes 786448 | tf_op jit(solution)/shard_map/reduce_scatter | solution.py:318
  841.8 41.9 %reduce-scatter.20.cloned.1.call-done = bf16[256,512]{1,0:T(8,128)(2,1)} async-done(((bf16[2048,512]{1,0:T(8,128)(2,1)}), bf16[256,512]{1,0:T(8,128)(2,1)}) %reduce-scatter.20.cloned.1.call-update) | async-done | bytes 262160 | tf_op jit(solution)/shard_map/reduce_scatter | solution.py:291
  885.5 42.6 %reduce-scatter.26.cloned.1.call-done = bf16[512,256]{1,0:T(8,128)(2,1)} async-done(((bf16[512,2048]{1,0:T(8,128)(2,1)}), bf16[512,256]{1,0:T(8,128)(2,1)}) %reduce-scatter.26.cloned.1.call-update) | async-done | bytes 262160 | tf_op jit(solution)/shard_map/reduce_scatter | solution.py:306
  929.9 44.0 %reduce-scatter.18.cloned.1.call-done = bf16[128,2048]{1,0:T(8,128)(2,1)} async-done(((bf16[512,2048]{1,0:T(8,128)(2,1)}), bf16[128,2048]{1,0:T(8,128)(2,1)}) %reduce-scatter.18.cloned.1.call-update) | async-done | bytes 524304 | tf_op jit(solution)/shard_map/reduce_scatter | solution.py:275
  975.4 13.8 %all-reduce.7 = (bf16[2048]{0:T(1024)(128)(2,1)S(1)}, bf16[128]{0:T(256)(128)(2,1)S(1)}, bf16[128]{0:T(256)(128)(2,1)S(1)}, bf16[2048]{0:T(1024)(128)(2,1)S(1)}) all-reduce(bf16[2048]{0:T(1024)(128)(2,1)S(1)} %get-tuple-element.68, bf16[128]{0:T(256)(128)(2,1)S(1)} %fusion.40, ...), channel_id=6, replica_groups=mesh['fsdp'=8,'tp'=4] {'fsdp'}, use_global_device_ids=true, to_apply=%region_18.19.clone | all-reduce | flops 4352 | bytes 17408
  989.3 11.8 %all-reduce.6 = (f32[256]{0:T(256)}, f32[16]{0:T(128)}, f32[16]{0:T(128)}, f32[256]{0:T(256)}) all-reduce(f32[256]{0:T(256)S(1)} %get-tuple-element.127, f32[16]{0:T(128)S(1)} %get-tuple-element.129, f32[16]{0:T(128)S(1)} %get-tuple-element.128, f32[256]{0:T(256)S(1)} %get-tuple-element.126), channel_id=1, replica_groups=mesh['fsdp'=8,'tp'=4] {'tp'}, use_global_device_ids=true, to_apply=%region_19.20 | all-reduce | flops 544 | bytes 4352 | tf_op jit(solution)/shard_map/psum | solution.py:324
  1001.1 18.2 %reduce-scatter.14.cloned.1.call-done = bf16[128,2048]{1,0:T(8,128)(2,1)} async-done(((bf16[512,2048]{1,0:T(8,128)(2,1)}), bf16[128,2048]{1,0:T(8,128)(2,1)}) %reduce-scatter.14.cloned.1.call-update) | async-done | bytes 524304 | tf_op jit(solution)/shard_map/reduce_scatter | solution.py:222
  (251 shorter events, 205.5 us)
Async XLA Ops:
  7.2 35.1 %all-gather.17.cloned.1.call-start = ((), (), s32[]{:S(2)}) async-start(), calls=%async_computation.14 | async-start | bytes 1179648 | tf_op jit(solution)/shard_map/all_gather | solution.py:167
  7.9 76.0 %all-gather.13.cloned.1.call-start = ((), (), s32[]{:S(2)}) async-start(), calls=%async_computation.12 | async-start | bytes 2621440 | tf_op jit(solution)/shard_map/all_gather | solution.py:183
  22.4 85.7 %all-gather.15.cloned.1.call-start = ((), (), s32[]{:S(2)}) async-start(), calls=%async_computation.13 | async-start | bytes 1179648 | tf_op jit(solution)/shard_map/all_gather | solution.py:168
  23.1 114.5 %all-gather.19.cloned.1.call-start = ((), (), s32[]{:S(2)}) async-start(), calls=%async_computation.15 | async-start | bytes 2359296 | tf_op jit(solution)/shard_map/all_gather | solution.py:166
  23.7 143.8 %all-gather.21.cloned.1.call-start = ((), (), s32[]{:S(2)}) async-start(), calls=%async_computation.16 | async-start | bytes 2359296 | tf_op jit(solution)/shard_map/all_gather | solution.py:171
  24.3 225.1 %reduce-scatter.12.cloned.1.call-start = ((), (), s32[]{:S(2)}) async-start(), calls=%async_computation.17 | async-start | bytes 5242880 | tf_op jit(solution)/shard_map/reduce_scatter | solution.py:204
  172.4 124.8 %all-gather.23.cloned.1.call-start = ((), (), s32[]{:S(2)}) async-start(), calls=%async_computation.18 | async-start | bytes 7077888 | tf_op jit(solution)/shard_map/all_gather | solution.py:175
  173.2 171.3 %all-gather.25.cloned.1.call-start = ((), (), s32[]{:S(2)}) async-start(), calls=%async_computation.19 | async-start | bytes 7077888 | tf_op jit(solution)/shard_map/all_gather | solution.py:176
  173.9 217.8 %all-gather.29.cloned.1.call-start = ((), (), s32[]{:S(2)}) async-start(), calls=%async_computation.22 | async-start | bytes 2621440 | tf_op jit(solution)/shard_map/all_gather | solution.py:229
  174.7 264.2 %all-gather.27.cloned.1.call-start = ((), (), s32[]{:S(2)}) async-start(), calls=%async_computation.20 | async-start | bytes 7077888 | tf_op jit(solution)/shard_map/all_gather | solution.py:177
  252.7 53.2 %all-to-all-start = ((bf16[4,128,2048]{2,1,0:T(8,128)(2,1)}), bf16[4,128,2048]{2,1,0:T(8,128)(2,1)}, u32[]{:S(2)}, u32[]{:S(2)}) async-start(bf16[4,128,2048]{2,1,0:T(8,128)(2,1)} %stack.2), calls=%async_computation.1 | async-start | bytes 4194304 | tf_op jit(solution)/shard_map/all_to_all | solution.py:215
  257.1 248.1 %reduce-scatter.16.cloned.1.call-start = ((), (), s32[]{:S(2)}) async-start(), calls=%async_computation.23 | async-start | bytes 2621440 | tf_op jit(solution)/shard_map/reduce_scatter | solution.py:238
  461.5 92.6 %all-gather.31.cloned.1.call-start = ((), (), s32[]{:S(2)}) async-start(), calls=%async_computation.24 | async-start | bytes 2621440 | tf_op jit(solution)/shard_map/all_gather | solution.py:249
  509.1 148.0 %reduce-scatter.22.cloned.1.call-start = ((), (), s32[]{:S(2)}) async-start(), calls=%async_computation.27 | async-start | bytes 1179648 | tf_op jit(solution)/shard_map/reduce_scatter | solution.py:294
  570.5 88.2 %reduce-scatter.24.cloned.1.call-start = ((), (), s32[]{:S(2)}) async-start(), calls=%async_computation.28 | async-start | bytes 1179648 | tf_op jit(solution)/shard_map/reduce_scatter | solution.py:297
  576.6 132.9 %reduce-scatter.28.cloned.1.call-start = ((), (), s32[]{:S(2)}) async-start(), calls=%async_computation.30 | async-start | bytes 7077888 | tf_op jit(solution)/shard_map/reduce_scatter | solution.py:312
  585.0 189.5 %reduce-scatter.30.cloned.1.call-start = ((), (), s32[]{:S(2)}) async-start(), calls=%async_computation.31 | async-start | bytes 7077888 | tf_op jit(solution)/shard_map/reduce_scatter | solution.py:315
  593.6 245.8 %reduce-scatter.32.cloned.1.call-start = ((), (), s32[]{:S(2)}) async-start(), calls=%async_computation.32 | async-start | bytes 7077888 | tf_op jit(solution)/shard_map/reduce_scatter | solution.py:318
  601.9 281.8 %reduce-scatter.20.cloned.1.call-start = ((), (), s32[]{:S(2)}) async-start(), calls=%async_computation.26 | async-start | bytes 2359296 | tf_op jit(solution)/shard_map/reduce_scatter | solution.py:291
  623.6 304.5 %reduce-scatter.26.cloned.1.call-start = ((), (), s32[]{:S(2)}) async-start(), calls=%async_computation.29 | async-start | bytes 2359296 | tf_op jit(solution)/shard_map/reduce_scatter | solution.py:306
  628.1 345.8 %reduce-scatter.18.cloned.1.call-start = ((), (), s32[]{:S(2)}) async-start(), calls=%async_computation.25 | async-start | bytes 2621440 | tf_op jit(solution)/shard_map/reduce_scatter | solution.py:275
  634.6 384.7 %reduce-scatter.14.cloned.1.call-start = ((), (), s32[]{:S(2)}) async-start(), calls=%async_computation.21 | async-start | bytes 2621440 | tf_op jit(solution)/shard_map/reduce_scatter | solution.py:222
  712.0 307.3 %copy-start.10 = (bf16[128,2048]{1,0:T(8,128)(2,1)S(1)}, bf16[128,2048]{1,0:T(8,128)(2,1)}, u32[]{:S(2)}) copy-start(bf16[128,2048]{1,0:T(8,128)(2,1)} %param.15) | copy-start | bytes 1572868
  712.0 307.3 %copy-start.18 = (bf16[128,2048]{1,0:T(8,128)(2,1)S(1)}, bf16[128,2048]{1,0:T(8,128)(2,1)}, u32[]{:S(2)}) copy-start(bf16[128,2048]{1,0:T(8,128)(2,1)} %reduce-scatter.16.cloned.1.call-done) | copy-start | bytes 1572868
  (47 other events, 352.1 us)
Sparse Core Ops, SparseCore 0:
  9.9 26.1 all-gather.16
  38.2 45.6 all-gather.12
  85.9 22.1 all-gather.14
  109.8 27.7 all-gather.18
  139.3 28.0 all-gather.20
  172.6 76.7 reduce-scatter.11
  251.3 45.8 all-gather.22
  299.1 45.3 all-gather.24
  346.1 45.6 all-gather.28
  393.5 45.3 all-gather.26
  461.6 43.6 reduce-scatter.15
  509.2 44.8 all-gather.30
  570.6 34.8 reduce-scatter.21
  608.5 35.9 reduce-scatter.23
  647.7 61.7 reduce-scatter.27
  712.8 61.7 reduce-scatter.29
  777.8 61.5 reduce-scatter.31
  842.5 41.1 reduce-scatter.19
  887.0 41.0 reduce-scatter.25
  930.2 43.5 reduce-scatter.17
  976.2 43.0 reduce-scatter.13
